TPU v7x, 256 devices: a whole 4x4x8 slice. The times are simulated.
256 devices in a mesh: row: 16 (over x, y_lo, core), col: 8 (over z), slab: 2 (over y_hi).
Axes of the slice: x: 4, y: 4 (y_hi: 2, y_lo: 2; y = y_hi * 2 + y_lo), z: 8, core: 2. Of those that a mesh axis runs over, the one named last changes fastest.
Arguments:
- fields: bfloat16 [2, 16384, 1024], P(None, ('row', 'col', 'slab')), may hold values from -0.8984375 to 0.8984375
Outputs:
- gram: float32 [2, 16384, 16384], P(None, ('row', 'slab'), 'col')
All inputs are finite; a program needn't handle non-finite values.
Results may differ from a plain program's by a relative error of at most 0.01.
Values may be sent and summed in bfloat16 or wider, within the bound.
A program may use at most 64 MiB of HBM per device.

v0:
```python
import jax
import jax.numpy as jnp
from jax import lax
from jax.sharding import PartitionSpec as P


def pair_terms(left_real, left_imag, piece):
    right_real = jnp.concatenate([piece[0], piece[1]], axis=1)
    right_imag = jnp.concatenate([piece[1], piece[0]], axis=1)
    dims = (((1,), (1,)), ((), ()))
    real = lax.dot_general(left_real, right_real, dims, preferred_element_type=jnp.float32)
    imag = lax.dot_general(left_imag, right_imag, dims, preferred_element_type=jnp.float32)
    return jnp.stack([real, imag])


def body(fields):
    local = lax.all_to_all(fields, "slab", split_axis=2, concat_axis=1, tiled=True)
    row_block = lax.all_gather(local, "col", axis=1, tiled=True)
    left_real = jnp.concatenate([row_block[0], row_block[1]], axis=1)
    left_imag = jnp.concatenate([row_block[0], -row_block[1]], axis=1)
    column_set = lax.all_gather(local, "row", axis=1, tiled=True)
    terms = pair_terms(left_real, left_imag, column_set)
    gram = lax.psum_scatter(
        terms.astype(jnp.bfloat16), "slab", scatter_dimension=1, tiled=True
    ).astype(jnp.float32)
    return gram


def solution(mesh):
    placed = (P(None, ("row", "col", "slab"), None),)
    return jax.shard_map(
        body, mesh=mesh, in_specs=placed, out_specs=P(None, ("row", "slab"), "col"), check_vma=False
    )
```

profile of v0, /device:TPU:1, one launch (start us, length us, event | category | flops | bytes accessed | tf_op | source)
XLA Modules:
  0.0 242.6 jit_solution(3190334933049715580)
XLA Ops:
  6.5 0.0 all-gather.3.cloned.1.call-start
  6.5 1.3 copy.3
  7.8 0.4 reshape
  8.2 10.3 %all_to_all.18 = bf16[2,2,32768]{2,1,0:T(2,128)(2,1)S(1)} all-to-all(bf16[2,2,32768]{2,1,0:T(2,128)(2,1)S(1)} %reshape), channel_id=1, replica_groups=mesh['row'=16,'col'=8,'slab'=2] {'slab'}, dimensions={0} | all-to-all | bytes 524288 | tf_op jit(solution)/shard_map/all_to_all | solution.py:17
  18.6 0.3 reshape.1
  18.9 1.0 copy.5
  19.9 0.0 all-gather.3.cloned.1.call-update
  19.9 0.0 all-gather.5.cloned.1.call-start
  20.0 0.7 all-gather.5.cloned.1.call-update
  20.7 0.0 reduce-scatter.2.cloned.1.call-start
  20.7 38.7 %all-gather.3.cloned.1.call-done = bf16[2,1024,512]{2,1,0:T(8,128)(2,1)} async-done(((bf16[2,128,512]{2,1,0:T(8,128)(2,1)}), bf16[2,1024,512]{2,1,0:T(8,128)(2,1)}) %all-gather.3.cloned.1.call-update) | async-done | bytes 2097168 | tf_op jit(solution)/shard_map/all_gather | solution.py:18
  59.4 1.3 fusion.16
  60.7 2.6 %slice_bitcast_fusion.2 = (bf16[1024,512]{1,0:T(8,128)(2,1)}, bf16[1024,512]{1,0:T(8,128)(2,1)S(1)}) fusion(bf16[2,1024,512]{2,1,0:T(8,128)(2,1)} %all-gather.3.cloned.1.call-done), kind=kLoop, calls=%fused_computation.17 | loop fusion | bytes 4194304 | tf_op jit(solution)/shard_map/squeeze | solution.py:19
  63.3 40.4 %all-gather.5.cloned.1.call-done = bf16[2,2048,512]{2,1,0:T(8,128)(2,1)} async-done(((bf16[2,128,512]{2,1,0:T(8,128)(2,1)}), bf16[2,2048,512]{2,1,0:T(8,128)(2,1)}) %all-gather.5.cloned.1.call-update) | async-done | bytes 4194320 | tf_op jit(solution)/shard_map/all_gather | solution.py:21
  103.8 0.0 copy-start
  103.8 2.6 %slice_bitcast_fusion = (bf16[2048,512]{1,0:T(8,128)(2,1)S(1)}, bf16[2048,512]{1,0:T(8,128)(2,1)S(1)}) fusion(bf16[2,2048,512]{2,1,0:T(8,128)(2,1)} %all-gather.5.cloned.1.call-done), kind=kLoop, calls=%fused_computation.13 | loop fusion | bytes 8388608 | tf_op jit(solution)/shard_map/squeeze | solution.py:8
  106.3 0.0 copy-done
  106.3 4.8 %convert_bitcast_fusion.1 = bf16[1,1024,2048]{2,1,0:T(8,128)(2,1)S(1)} fusion(bf16[2048,512]{1,0:T(8,128)(2,1)S(1)} %get-tuple-element.5, bf16[2048,512]{1,0:T(8,128)(2,1)S(1)} %get-tuple-element.6, bf16[1024,512]{1,0:T(8,128)(2,1)S(1)} %get-tuple-element.8, bf16[1024,512]{1,0:T(8,128)(2,1)S(1)} %copy-done), kind=kOutput, calls=%fused_computation.10 | convolution fusion | flops 4309647360 | bytes 10485760 | tf_op jit(solution)/shard_map/dot_general | solution.py:11
  111.1 6.1 %convert_bitcast_fusion = bf16[1,1024,2048]{2,1,0:T(8,128)(2,1)} fusion(bf16[2048,512]{1,0:T(8,128)(2,1)S(1)} %get-tuple-element.6, bf16[2048,512]{1,0:T(8,128)(2,1)S(1)} %get-tuple-element.5, bf16[1024,512]{1,0:T(8,128)(2,1)S(1)} %get-tuple-element.8, bf16[1024,512]{1,0:T(8,128)(2,1)S(1)} %fusion.16), kind=kOutput, calls=%fused_computation.9 | convolution fusion | flops 4309647360 | bytes 10485760 | tf_op jit(solution)/shard_map/dot_general | solution.py:12
  117.3 6.3 %pad_maximum_fusion = bf16[2,1024,2048]{2,1,0:T(8,128)(2,1)} fusion(bf16[1,1024,2048]{2,1,0:T(8,128)(2,1)} %convert_bitcast_fusion, bf16[1,1024,2048]{2,1,0:T(8,128)(2,1)S(1)} %convert_bitcast_fusion.1), kind=kLoop, calls=%fused_computation | loop fusion | flops 4194304 | bytes 16777216 | tf_op jit(solution)/shard_map/stack | solution.py:13
  123.6 0.0 reduce-scatter.2.cloned.1.call-update
  123.6 105.7 %reduce-scatter.2.cloned.1.call-done = bf16[2,512,2048]{2,1,0:T(8,128)(2,1)} async-done(((bf16[2,1024,2048]{2,1,0:T(8,128)(2,1)}), bf16[2,512,2048]{2,1,0:T(8,128)(2,1)}) %reduce-scatter.2.cloned.1.call-update) | async-done | bytes 4194320 | tf_op jit(solution)/shard_map/reduce_scatter | solution.py:23
  229.4 6.7 %convert_element_type.4 = f32[2,512,2048]{2,1,0:T(8,128)} convert(bf16[2,512,2048]{2,1,0:T(8,128)(2,1)} %reduce-scatter.2.cloned.1.call-done) | non-fusion elementwise | flops 2097152 | bytes 12582912 | tf_op jit(solution)/shard_map/convert_element_type | solution.py:25
Async XLA Ops:
  6.5 52.9 %all-gather.3.cloned.1.call-start = ((), (), s32[]{:S(2)}) async-start(), calls=%async_computation.2 | async-start | bytes 2359296 | tf_op jit(solution)/shard_map/all_gather | solution.py:18
  19.9 83.8 %all-gather.5.cloned.1.call-start = ((), (), s32[]{:S(2)}) async-start(), calls=%async_computation.3 | async-start | bytes 4456448 | tf_op jit(solution)/shard_map/all_gather | solution.py:21
  20.7 208.7 %reduce-scatter.2.cloned.1.call-start = ((), (), s32[]{:S(2)}) async-start(), calls=%async_computation.4 | async-start | bytes 12582912 | tf_op jit(solution)/shard_map/reduce_scatter | solution.py:23
  103.8 2.6 %copy-start = (bf16[1024,512]{1,0:T(8,128)(2,1)S(1)}, bf16[1024,512]{1,0:T(8,128)(2,1)}, u32[]{:S(2)}) copy-start(bf16[1024,512]{1,0:T(8,128)(2,1)} %get-tuple-element.7) | copy-start | bytes 3145732
Sparse Core Ops, SparseCore 0:
  20.1 39.2 all-gather.2
  61.2 42.4 all-gather.4
  123.8 105.5 reduce-scatter.1
where the time goes:
time: 243 us
  waiting for transfers between devices  186 us (77%)
  other arithmetic  14.3 us (6%)
  between operations  13.2 us (5%)
  matrix products  10.9 us (4%)
  blocking collectives  10.3 us (4%)
  local copies, waits for them, and re-layouts  8.25 us (3%)
    reduce_scatter x1, waiting for transfers between devices, body(): lax.psum_scatter(terms.astype(jnp.bfloat16), 'slab', scatter_dimension=1,...  106 us
    all_gather x1, waiting for transfers between devices, body(): column_set = lax.all_gather(local, 'row', axis=1, tiled=True)  40.4 us
    all_gather x1, waiting for transfers between devices, body(): row_block = lax.all_gather(local, 'col', axis=1, tiled=True)  38.7 us
    all_to_all x1, blocking collectives, body(): lax.all_to_all(fields, 'slab', split_axis=2, concat_axis=1, tiled=True)  10.3 us
    convert_element_type x1, other arithmetic, body(): gram = lax.psum_scatter(terms.astype(jnp.bfloat16), 'slab', scatter_dimen...  6.65 us
    another operation x1, other arithmetic, pair_terms(): return jnp.stack([real, imag])  6.35 us
    dot_general x1, matrix products, pair_terms(): lax.dot_general(left_imag, right_imag, dims, preferred_element_type=jnp.f...  6.13 us
  transfers between devices with their start and end apart: 3, of which 3 were waited for; matrix products, arithmetic and copies ran while one was open for 2% of the time, Pallas kernels for 0%

commit v1 on v0

--- a/solution.py
+++ b/solution.py
@@ -15,7 +15,12 @@
 
 def body(fields):
     local = lax.all_to_all(fields, "slab", split_axis=2, concat_axis=1, tiled=True)
-    row_block = lax.all_gather(local, "col", axis=1, tiled=True)
+    ring = [local]
+    for hop in range(7):
+        ring.append(lax.ppermute(ring[-1], "col", [(dev, (dev + 1) % 8) for dev in range(8)]))
+    row_block = jnp.roll(
+        jnp.concatenate(ring[::-1], axis=1), (lax.axis_index("col") + 1) * ring[0].shape[1], axis=1
+    )
     left_real = jnp.concatenate([row_block[0], row_block[1]], axis=1)
     left_imag = jnp.concatenate([row_block[0], -row_block[1]], axis=1)
     column_set = lax.all_gather(local, "row", axis=1, tiled=True)

time: 243 us -> 225 us (0.926)
  waiting for transfers between devices: 186 us -> 167 us
    ppermute x0 -> x7, waiting for transfers between devices: none -> 54.8 us  [body(): lax.ppermute(ring[-1], 'col', [(dev, (dev + 1) % 8) for dev in range(8)])]
    all_gather x1, waiting for transfers between devices: 40.4 us -> 0.01 us  [body(): column_set = lax.all_gather(local, 'row', axis=1, tiled=True)]
    all_gather x1 -> x0, waiting for transfers between devices: 38.7 us -> none  [body(): row_block = lax.all_gather(local, 'col', axis=1, tiled=True)]
    reduce_scatter x1, waiting for transfers between devices: 106 us -> 112 us  [body(): lax.psum_scatter(terms.astype(jnp.bfloat16), 'slab', scatter_dimension=1,...]
    squeeze x1, local copies, waits for them, and re-layouts: 2.65 us -> 0.08 us  [body(): left_real = jnp.concatenate([row_block[0], row_block[1]], axis=1)]
  transfers between devices with their start and end apart: 3 -> 9, of which waited for: 3 -> 8; matrix products, arithmetic and copies ran while one was open for 2% -> 1% of each run, Pallas kernels for 0% -> 0%
where the time goes in v1:
time: 225 us
  waiting for transfers between devices  167 us (74%)
  other arithmetic  14.3 us (6%)
  between operations  13.6 us (6%)
  matrix products  10.9 us (5%)
  blocking collectives  10.3 us (5%)
  local copies, waits for them, and re-layouts  6.98 us (3%)
    reduce_scatter x1, waiting for transfers between devices, body(): lax.psum_scatter(terms.astype(jnp.bfloat16), 'slab', scatter_dimension=1,...  112 us
    ppermute x7, waiting for transfers between devices, body(): lax.ppermute(ring[-1], 'col', [(dev, (dev + 1) % 8) for dev in range(8)])  54.8 us
    all_to_all x1, blocking collectives, body(): lax.all_to_all(fields, 'slab', split_axis=2, concat_axis=1, tiled=True)  10.3 us
    convert_element_type x1, other arithmetic, body(): gram = lax.psum_scatter(terms.astype(jnp.bfloat16), 'slab', scatter_dimen...  6.65 us
    another operation x1, other arithmetic, pair_terms(): return jnp.stack([real, imag])  6.35 us
    dot_general x1, matrix products, pair_terms(): lax.dot_general(left_real, right_real, dims, preferred_element_type=jnp.f...  6.12 us
    dot_general x1, matrix products, pair_terms(): lax.dot_general(left_imag, right_imag, dims, preferred_element_type=jnp.f...  4.78 us
  transfers between devices with their start and end apart: 9, of which 8 were waited for; matrix products, arithmetic and copies ran while one was open for 1% of the time, Pallas kernels for 0%

profile of v1, /device:TPU:1, one launch (start us, length us, event | category | flops | bytes accessed | tf_op | source)
XLA Modules:
  0.0 224.6 jit_solution(3037738291926880050)
XLA Ops:
  6.5 1.3 copy.3
  7.8 0.4 reshape
  8.2 10.3 %all_to_all.18 = bf16[2,2,32768]{2,1,0:T(2,128)(2,1)S(1)} all-to-all(bf16[2,2,32768]{2,1,0:T(2,128)(2,1)S(1)} %reshape), channel_id=1, replica_groups=mesh['row'=16,'col'=8,'slab'=2] {'slab'}, dimensions={0} | all-to-all | bytes 524288 | tf_op jit(solution)/shard_map/all_to_all | solution.py:17
  18.5 0.3 reshape.1
  18.9 1.0 copy.5
  20.0 0.0 all-gather.2.cloned.1.call-update
  20.0 0.0 reduce-scatter.2.cloned.1.call-start
  20.0 1.7 collective-permute-start
  21.7 8.7 %collective-permute-done = bf16[2,128,512]{2,1,0:T(8,128)(2,1)S(1)} collective-permute-done((bf16[2,128,512]{2,1,0:T(8,128)(2,1)}, bf16[2,128,512]{2,1,0:T(8,128)(2,1)S(1)}, u32[]{:S(2)}, u32[]{:S(2)}) %collective-permute-start) | collective-permute-done | bytes 262176 | tf_op jit(solution)/shard_map/ppermute | solution.py:20
  30.4 0.0 collective-permute-start.1
  30.4 6.4 %collective-permute-done.1 = bf16[2,128,512]{2,1,0:T(8,128)(2,1)S(1)} collective-permute-done((bf16[2,128,512]{2,1,0:T(8,128)(2,1)S(1)}, bf16[2,128,512]{2,1,0:T(8,128)(2,1)S(1)}, u32[]{:S(2)}, u32[]{:S(2)}) %collective-permute-start.1) | collective-permute-done | bytes 262176 | tf_op jit(solution)/shard_map/ppermute | solution.py:20
  36.8 0.0 collective-permute-start.2
  36.8 6.4 %collective-permute-done.2 = bf16[2,128,512]{2,1,0:T(8,128)(2,1)S(1)} collective-permute-done((bf16[2,128,512]{2,1,0:T(8,128)(2,1)S(1)}, bf16[2,128,512]{2,1,0:T(8,128)(2,1)S(1)}, u32[]{:S(2)}, u32[]{:S(2)}) %collective-permute-start.2) | collective-permute-done | bytes 262176 | tf_op jit(solution)/shard_map/ppermute | solution.py:20
  43.3 0.0 collective-permute-start.3
  43.3 7.2 %collective-permute-done.3 = bf16[2,128,512]{2,1,0:T(8,128)(2,1)S(1)} collective-permute-done((bf16[2,128,512]{2,1,0:T(8,128)(2,1)S(1)}, bf16[2,128,512]{2,1,0:T(8,128)(2,1)S(1)}, u32[]{:S(2)}, u32[]{:S(2)}) %collective-permute-start.3) | collective-permute-done | bytes 262176 | tf_op jit(solution)/shard_map/ppermute | solution.py:20
  50.4 0.0 collective-permute-start.4
  50.4 8.2 %collective-permute-done.4 = bf16[2,128,512]{2,1,0:T(8,128)(2,1)S(1)} collective-permute-done((bf16[2,128,512]{2,1,0:T(8,128)(2,1)S(1)}, bf16[2,128,512]{2,1,0:T(8,128)(2,1)S(1)}, u32[]{:S(2)}, u32[]{:S(2)}) %collective-permute-start.4) | collective-permute-done | bytes 262176 | tf_op jit(solution)/shard_map/ppermute | solution.py:20
  58.7 0.0 collective-permute-start.5
  58.7 9.4 %collective-permute-done.5 = bf16[2,128,512]{2,1,0:T(8,128)(2,1)S(1)} collective-permute-done((bf16[2,128,512]{2,1,0:T(8,128)(2,1)S(1)}, bf16[2,128,512]{2,1,0:T(8,128)(2,1)S(1)}, u32[]{:S(2)}, u32[]{:S(2)}) %collective-permute-start.5) | collective-permute-done | bytes 262176 | tf_op jit(solution)/shard_map/ppermute | solution.py:20
  68.1 0.0 collective-permute-start.6
  68.1 8.5 %collective-permute-done.6 = bf16[2,128,512]{2,1,0:T(8,128)(2,1)S(1)} collective-permute-done((bf16[2,128,512]{2,1,0:T(8,128)(2,1)S(1)}, bf16[2,128,512]{2,1,0:T(8,128)(2,1)S(1)}, u32[]{:S(2)}, u32[]{:S(2)}) %collective-permute-start.6) | collective-permute-done | bytes 262176 | tf_op jit(solution)/shard_map/ppermute | solution.py:20
  76.8 1.0 constant_dynamic-update-slice_fusion.8
  78.0 0.1 dynamic-slice_bitcast_fusion.1
  78.1 1.3 fusion.16
  79.3 2.6 %slice_bitcast_fusion = (bf16[2048,512]{1,0:T(8,128)(2,1)S(1)}, bf16[2048,512]{1,0:T(8,128)(2,1)S(1)}) fusion(bf16[2,2048,512]{2,1,0:T(8,128)(2,1)} %all-gather.2.cloned.1.call-done), kind=kLoop, calls=%fused_computation.13 | loop fusion | bytes 8388608 | tf_op jit(solution)/shard_map/squeeze | solution.py:8
  81.9 0.0 copy-done.1
  81.9 4.8 %convert_bitcast_fusion = bf16[1,1024,2048]{2,1,0:T(8,128)(2,1)S(1)} fusion(bf16[2048,512]{1,0:T(8,128)(2,1)S(1)} %get-tuple-element.8, bf16[2048,512]{1,0:T(8,128)(2,1)S(1)} %get-tuple-element.7, bf16[1024,512]{1,0:T(8,128)(2,1)S(1)} %dynamic-slice_bitcast_fusion.1, bf16[1024,512]{1,0:T(8,128)(2,1)S(1)} %copy-done.1), kind=kOutput, calls=%fused_computation.9 | convolution fusion | flops 4309647360 | bytes 10485760 | tf_op jit(solution)/shard_map/dot_general | solution.py:12
  86.7 6.1 %convert_bitcast_fusion.1 = bf16[1,1024,2048]{2,1,0:T(8,128)(2,1)} fusion(bf16[2048,512]{1,0:T(8,128)(2,1)S(1)} %get-tuple-element.7, bf16[2048,512]{1,0:T(8,128)(2,1)S(1)} %get-tuple-element.8, bf16[1024,512]{1,0:T(8,128)(2,1)S(1)} %dynamic-slice_bitcast_fusion.1, bf16[1024,512]{1,0:T(8,128)(2,1)S(1)} %get-tuple-element.6), kind=kOutput, calls=%fused_computation.10 | convolution fusion | flops 4309647360 | bytes 10485760 | tf_op jit(solution)/shard_map/dot_general | solution.py:11
  92.8 6.3 %pad_maximum_fusion = bf16[2,1024,2048]{2,1,0:T(8,128)(2,1)} fusion(bf16[1,1024,2048]{2,1,0:T(8,128)(2,1)S(1)} %convert_bitcast_fusion, bf16[1,1024,2048]{2,1,0:T(8,128)(2,1)} %convert_bitcast_fusion.1), kind=kLoop, calls=%fused_computation | loop fusion | flops 4194304 | bytes 16777216 | tf_op jit(solution)/shard_map/stack | solution.py:13
  99.2 0.0 reduce-scatter.2.cloned.1.call-update
  99.2 111.9 %reduce-scatter.2.cloned.1.call-done = bf16[2,512,2048]{2,1,0:T(8,128)(2,1)} async-done(((bf16[2,1024,2048]{2,1,0:T(8,128)(2,1)}), bf16[2,512,2048]{2,1,0:T(8,128)(2,1)}) %reduce-scatter.2.cloned.1.call-update) | async-done | bytes 4194320 | tf_op jit(solution)/shard_map/reduce_scatter | solution.py:28
  211.1 6.7 %convert_element_type.4 = f32[2,512,2048]{2,1,0:T(8,128)} convert(bf16[2,512,2048]{2,1,0:T(8,128)(2,1)} %reduce-scatter.2.cloned.1.call-done) | non-fusion elementwise | flops 2097152 | bytes 12582912 | tf_op jit(solution)/shard_map/convert_element_type | solution.py:30
  (20 shorter events, 0.3 us)
Async XLA Ops:
  6.5 72.8 %all-gather.2.cloned.1.call-start = ((), (), s32[]{:S(2)}) async-start(), calls=%async_computation.2 | async-start | bytes 4456448 | tf_op jit(solution)/shard_map/all_gather | solution.py:26
  20.0 58.0 %copy-start = (bf16[2,2,64,512]{3,2,1,0:T(8,128)(2,1)S(1)}, bf16[2,2,64,512]{3,2,1,0:T(8,128)(2,1)}, u32[]{:S(2)}) copy-start(bf16[2,2,64,512]{3,2,1,0:T(8,128)(2,1)} %copy.5) | copy-start | bytes 786436
  20.0 191.2 %reduce-scatter.2.cloned.1.call-start = ((), (), s32[]{:S(2)}) async-start(), calls=%async_computation.3 | async-start | bytes 12582912 | tf_op jit(solution)/shard_map/reduce_scatter | solution.py:28
  20.0 10.4 %collective-permute-start = (bf16[2,128,512]{2,1,0:T(8,128)(2,1)}, bf16[2,128,512]{2,1,0:T(8,128)(2,1)S(1)}, u32[]{:S(2)}, u32[]{:S(2)}) collective-permute-start(bf16[2,128,512]{2,1,0:T(8,128)(2,1)} %bitcast.21), channel_id=1, source_target_pairs={{0,2},{2,4},{4,6},{6,8},{8,10},{10,12},{12,14},{14,0},{1,3},{3,5},... | collective-permute-start | bytes 786440 | tf_op jit(solution)/shard_map/ppermute | solution.py:20
  30.4 6.4 %collective-permute-start.1 = (bf16[2,128,512]{2,1,0:T(8,128)(2,1)S(1)}, bf16[2,128,512]{2,1,0:T(8,128)(2,1)S(1)}, u32[]{:S(2)}, u32[]{:S(2)}) collective-permute-start(bf16[2,128,512]{2,1,0:T(8,128)(2,1)S(1)} %collective-permute-done), channel_id=1, source_target_pairs={{0,2},{2,4},{4,6},{6,8},{8,10},{10,12},{12,14},{14,0},{1,3},{3,5},... | collective-permute-start | bytes 786440 | tf_op jit(solution)/shard_map/ppermute | solution.py:20
  36.8 6.4 %collective-permute-start.2 = (bf16[2,128,512]{2,1,0:T(8,128)(2,1)S(1)}, bf16[2,128,512]{2,1,0:T(8,128)(2,1)S(1)}, u32[]{:S(2)}, u32[]{:S(2)}) collective-permute-start(bf16[2,128,512]{2,1,0:T(8,128)(2,1)S(1)} %collective-permute-done.1), channel_id=1, source_target_pairs={{0,2},{2,4},{4,6},{6,8},{8,10},{10,12},{12,14},{14,0},{1,3},{3,5},... | collective-permute-start | bytes 786440 | tf_op jit(solution)/shard_map/ppermute | solution.py:20
  43.3 7.2 %collective-permute-start.3 = (bf16[2,128,512]{2,1,0:T(8,128)(2,1)S(1)}, bf16[2,128,512]{2,1,0:T(8,128)(2,1)S(1)}, u32[]{:S(2)}, u32[]{:S(2)}) collective-permute-start(bf16[2,128,512]{2,1,0:T(8,128)(2,1)S(1)} %collective-permute-done.2), channel_id=1, source_target_pairs={{0,2},{2,4},{4,6},{6,8},{8,10},{10,12},{12,14},{14,0},{1,3},{3,5},... | collective-permute-start | bytes 786440 | tf_op jit(solution)/shard_map/ppermute | solution.py:20
  50.4 8.2 %collective-permute-start.4 = (bf16[2,128,512]{2,1,0:T(8,128)(2,1)S(1)}, bf16[2,128,512]{2,1,0:T(8,128)(2,1)S(1)}, u32[]{:S(2)}, u32[]{:S(2)}) collective-permute-start(bf16[2,128,512]{2,1,0:T(8,128)(2,1)S(1)} %collective-permute-done.3), channel_id=1, source_target_pairs={{0,2},{2,4},{4,6},{6,8},{8,10},{10,12},{12,14},{14,0},{1,3},{3,5},... | collective-permute-start | bytes 786440 | tf_op jit(solution)/shard_map/ppermute | solution.py:20
  58.7 9.4 %collective-permute-start.5 = (bf16[2,128,512]{2,1,0:T(8,128)(2,1)S(1)}, bf16[2,128,512]{2,1,0:T(8,128)(2,1)S(1)}, u32[]{:S(2)}, u32[]{:S(2)}) collective-permute-start(bf16[2,128,512]{2,1,0:T(8,128)(2,1)S(1)} %collective-permute-done.4), channel_id=1, source_target_pairs={{0,2},{2,4},{4,6},{6,8},{8,10},{10,12},{12,14},{14,0},{1,3},{3,5},... | collective-permute-start | bytes 786440 | tf_op jit(solution)/shard_map/ppermute | solution.py:20
  68.1 8.5 %collective-permute-start.6 = (bf16[2,128,512]{2,1,0:T(8,128)(2,1)S(1)}, bf16[2,128,512]{2,1,0:T(8,128)(2,1)S(1)}, u32[]{:S(2)}, u32[]{:S(2)}) collective-permute-start(bf16[2,128,512]{2,1,0:T(8,128)(2,1)S(1)} %collective-permute-done.5), channel_id=1, source_target_pairs={{0,2},{2,4},{4,6},{6,8},{8,10},{10,12},{12,14},{14,0},{1,3},{3,5},... | collective-permute-start | bytes 786440 | tf_op jit(solution)/shard_map/ppermute | solution.py:20
  79.3 2.6 %copy-start.1 = (bf16[1024,512]{1,0:T(8,128)(2,1)S(1)}, bf16[1024,512]{1,0:T(8,128)(2,1)}, u32[]{:S(2)}) copy-start(bf16[1024,512]{1,0:T(8,128)(2,1)} %get-tuple-element.5) | copy-start | bytes 3145732
Sparse Core Ops, SparseCore 0:
  20.1 42.1 all-gather.1
  99.3 111.7 reduce-scatter.1
